TPU v7x, 32 devices: a whole 2x2x4 slice. The times are simulated.
32 devices in a mesh: pair: 4 (over x, core), blk: 8 (over z, y).
Axes of the slice: x: 2, y: 2, z: 4, core: 2. Of those that a mesh axis runs over, the one named last changes fastest.
Arguments:
- left_feats: bfloat16 [4, 64, 256, 256], P('pair', None, 'blk'), may hold values from -6 to 6
- right_feats: bfloat16 [4, 64, 256, 256], P('pair', None, 'blk'), may hold values from -6 to 6
- offsets: int32 [8], P('blk'), may hold values from 0 to 3, as said below
- hidden: bfloat16 [4, 64, 256, 128], P('pair', None, 'blk'), may hold values from -1 to 1
- context: bfloat16 [4, 3, 64, 256, 128], P('pair', None, None, 'blk'), may hold values from -6 to 6
- gru_weights: bfloat16 [2, 3, 5, 164, 128], replicated, may hold values from -0.21875 to 0.21875
- hidden_grad: float32 [4, 64, 256, 128], P('pair', None, 'blk'), may hold values from -0.06 to 0.06
Outputs:
- new_hidden: bfloat16 [4, 64, 256, 128], P('pair', None, 'blk')
- weight_grads: float32 [2, 3, 5, 164, 128], replicated
- hidden_in_grad: float32 [4, 64, 256, 128], P('pair', None, 'blk')
Inputs may be any that keep to these rules, and one draw needn't show every extreme that they name: Stripe s reads the frame-2 blocks s - offsets[s] - 1 and s - offsets[s]; some stripe has offset 4 - 1.
All inputs are finite; a program needn't handle non-finite values.
Results may differ from a plain program's by a relative error of at most 0.0054.
Values may be sent and summed in bfloat16 or wider, within the bound.
A program may use at most 128 MiB of HBM per device.

v0:
```python
import functools
import math
import jax
import jax.numpy as jnp
import numpy as np
from jax import lax
from jax.sharding import PartitionSpec as P

LEVELS = 4
RADIUS = 4


def with_halo(block, sides, width):
    for axis, dim in sides:
        count = lax.axis_size(axis)
        forward = [(i, i + 1) for i in range(count - 1)]
        backward = [(target, source) for source, target in forward]
        low = lax.ppermute(
            lax.slice_in_dim(block, block.shape[dim] - width, None, axis=dim), axis, forward
        )
        high = lax.ppermute(lax.slice_in_dim(block, 0, width, axis=dim), axis, backward)
        block = jnp.concatenate([low, block, high], axis=dim)
    return block


def lookup_table(column_count, level_count, radius_len):
    tap_count = 2 * radius_len + 1
    lookup = np.zeros((column_count, 2 * column_count, level_count * tap_count), np.float32)
    positions = np.arange(column_count)
    for level_id in range(level_count):
        pool_span = 2**level_id
        pooled_cols = 2 * column_count // pool_span
        for tap_id in range(tap_count):
            centre = (positions + column_count // 2) // pool_span + tap_id - radius_len
            inside = (centre >= 0) & (centre < pooled_cols)
            for inner_id in range(pool_span):
                lookup[
                    positions[inside],
                    centre[inside] * pool_span + inner_id,
                    level_id * tap_count + tap_id,
                ] = (1.0 / pool_span)
    return lookup


def tap_stack(padded, extent, axis_dim, kernel_len):
    return jnp.concatenate(
        [
            lax.slice_in_dim(padded, tap_id, tap_id + extent, axis=axis_dim)
            for tap_id in range(kernel_len)
        ],
        axis=-1,
    )


def conv_apply(padded, weight_taps, extent, axis_dim):
    kernel_len, in_chan, out_chan = weight_taps.shape
    stacked = tap_stack(padded, extent, axis_dim, kernel_len)
    flat_taps = stacked.reshape(-1, kernel_len * in_chan)
    result = jnp.dot(
        flat_taps,
        weight_taps.reshape(kernel_len * in_chan, out_chan),
        preferred_element_type=jnp.float32,
    )
    return result.reshape(stacked.shape[:-1] + (out_chan,))


def conv_weight_grad(padded, deltas, axis_dim):
    extent = deltas.shape[axis_dim]
    kernel_len = padded.shape[axis_dim] - extent + 1
    stacked = tap_stack(padded, extent, axis_dim, kernel_len)
    flat_taps = stacked.reshape(-1, stacked.shape[-1])
    flat_deltas = deltas.reshape(-1, deltas.shape[-1])
    result = lax.dot_general(
        flat_taps, flat_deltas, (((0,), (0,)), ((), ())), preferred_element_type=jnp.float32
    )
    return result.reshape(kernel_len, padded.shape[-1], deltas.shape[-1])


def conv_input_grad(deltas, weight_taps, axis_dim):
    kernel_len, in_chan, out_chan = weight_taps.shape
    backward_taps = lax.dot_general(
        deltas.reshape(-1, out_chan),
        weight_taps.reshape(kernel_len * in_chan, out_chan),
        (((1,), (1,)), ((), ())),
        preferred_element_type=jnp.float32,
    )
    backward_taps = backward_taps.reshape(deltas.shape[:-1] + (kernel_len * in_chan,))
    summed = None
    for tap_id in range(kernel_len):
        tap_part = backward_taps[..., tap_id * in_chan : (tap_id + 1) * in_chan]
        widths = [(0, 0)] * deltas.ndim
        widths[axis_dim] = (tap_id, kernel_len - 1 - tap_id)
        shifted = jnp.pad(tap_part, widths)
        summed = shifted if summed is None else summed + shifted
    return summed


def pad_along(values, axis_dim):
    widths = [(0, 0)] * values.ndim
    widths[axis_dim] = (2, 2)
    return jnp.pad(values, widths)


def crop_along(values, axis_dim):
    extent = values.shape[axis_dim] - 4
    return lax.slice_in_dim(values, 2, extent + 2, axis=axis_dim)


def section_forward(padded, context_parts, weights, axis_dim, extend):
    extent = padded.shape[axis_dim] - 4
    hidden_width = weights.shape[-1]
    own_inputs = lax.slice_in_dim(padded, 2, extent + 2, axis=axis_dim)
    hidden_own = own_inputs[..., :hidden_width].astype(jnp.float32)
    feat_padded = padded[..., hidden_width:]
    update_gate = jax.nn.sigmoid(
        conv_apply(padded, weights[0], extent, axis_dim) + context_parts[0].astype(jnp.float32)
    )
    reset_gate = jax.nn.sigmoid(
        conv_apply(padded, weights[1], extent, axis_dim) + context_parts[1].astype(jnp.float32)
    )
    reset_hidden = (reset_gate * hidden_own).astype(jnp.bfloat16)
    gated_padded = jnp.concatenate([extend(reset_hidden), feat_padded], axis=-1)
    candidate = jnp.tanh(
        conv_apply(gated_padded, weights[2], extent, axis_dim)
        + context_parts[2].astype(jnp.float32)
    )
    blended = (1.0 - update_gate) * hidden_own + update_gate * candidate
    return (blended, (update_gate, reset_gate, candidate, hidden_own, padded, gated_padded))


def section_backward(cotangent, stored, weights, axis_dim, fold_rims):
    update_gate, reset_gate, candidate, hidden_own, padded, gated_padded = stored
    hidden_width = weights.shape[-1]
    delta_cand = (cotangent * update_gate * (1.0 - candidate * candidate)).astype(jnp.bfloat16)
    grad_cand = conv_weight_grad(gated_padded, delta_cand, axis_dim)
    back_gated = fold_rims(conv_input_grad(delta_cand, weights[2][:, :hidden_width], axis_dim))
    delta_update = (
        cotangent * (candidate - hidden_own) * update_gate * (1.0 - update_gate)
    ).astype(jnp.bfloat16)
    delta_reset = (back_gated * hidden_own * reset_gate * (1.0 - reset_gate)).astype(jnp.bfloat16)
    grad_update = conv_weight_grad(padded, delta_update, axis_dim)
    grad_reset = conv_weight_grad(padded, delta_reset, axis_dim)
    grad_stack = jnp.stack([grad_update, grad_reset, grad_cand])
    back_inputs = conv_input_grad(
        delta_update, weights[0][:, :hidden_width], axis_dim
    ) + conv_input_grad(delta_reset, weights[1][:, :hidden_width], axis_dim)
    hidden_back = cotangent * (1.0 - update_gate) + back_gated * reset_gate + fold_rims(back_inputs)
    return (grad_stack, hidden_back)


def extend_gated(values):
    return with_halo(values, (("blk", 1),), 2)


def stripe_rims(values):
    extent = values.shape[1] - 4
    edge_terms = jnp.concatenate([values[:, :2], values[:, extent + 2 :]], axis=1)
    arrived = with_halo(edge_terms, (("blk", 1),), 2)
    own_terms = values[:, 2 : extent + 2]
    from_left = jnp.pad(arrived[:, :2], ((0, 0), (0, extent - 2), (0, 0)))
    from_right = jnp.pad(arrived[:, 6:], ((0, 0), (extent - 2, 0), (0, 0)))
    return own_terms + from_left + from_right


def on_device(left_feats, right_feats, offsets, hidden, context, gru_weights, hidden_grad):
    left_block = left_feats[0]
    right_block = right_feats[0]
    offset = offsets[0]
    stripe = lax.axis_index("blk")
    column_count = left_block.shape[1]
    empty_block = jnp.zeros_like(right_block)
    low_id = stripe - offset - 1
    high_id = stripe - offset
    shards = lax.all_gather(right_block, "blk", axis=1, tiled=True)
    shard_cols = shards.shape[1]

    def pick_one(slot_block, block_id):
        local_col = block_id * column_count
        usable = (local_col >= 0) & (local_col + column_count <= shard_cols)
        picked = lax.dynamic_slice_in_dim(
            shards, jnp.clip(local_col, 0, shard_cols - column_count), column_count, 1
        )
        return jnp.where(usable, picked, slot_block)

    low_block = pick_one(empty_block, low_id)
    high_block = pick_one(empty_block, high_id)
    window = jnp.concatenate([low_block, high_block], axis=1)
    scores = jnp.einsum("hxc,hjc->hxj", left_block, window, preferred_element_type=jnp.float32) * (
        1.0 / math.sqrt(left_block.shape[-1])
    )
    lookup = jnp.asarray(lookup_table(column_count, LEVELS, RADIUS))
    features = jnp.einsum("hxj,xjf->hxf", scores, lookup, precision=lax.Precision.HIGHEST).astype(
        jnp.bfloat16
    )
    context_parts = context[0]
    first_inputs = jnp.concatenate([hidden[0], features], axis=-1)
    first_padded = with_halo(first_inputs, (("blk", 1),), 2)
    first_new, first_stored = section_forward(
        first_padded, context_parts, gru_weights[0], 1, extend_gated
    )
    first_hidden = first_new.astype(jnp.bfloat16)
    second_inputs = jnp.concatenate([first_hidden, features], axis=-1)
    second_new, second_stored = section_forward(
        pad_along(second_inputs, 0),
        context_parts,
        gru_weights[1],
        0,
        functools.partial(pad_along, axis_dim=0),
    )
    second_grads, first_back = section_backward(
        hidden_grad[0], second_stored, gru_weights[1], 0, functools.partial(crop_along, axis_dim=0)
    )
    first_grads, hidden_back = section_backward(
        first_back, first_stored, gru_weights[0], 1, stripe_rims
    )
    grad_stack = lax.psum(jnp.stack([first_grads, second_grads]), ("pair", "blk"))
    return (second_new.astype(jnp.bfloat16)[None], grad_stack, hidden_back[None])


def solution(mesh):
    placed = (
        P("pair", None, "blk", None),
        P("pair", None, "blk", None),
        P("blk"),
        P("pair", None, "blk", None),
        P("pair", None, None, "blk", None),
        P(),
        P("pair", None, "blk", None),
    )
    return jax.shard_map(
        on_device,
        mesh=mesh,
        in_specs=placed,
        out_specs=(P("pair", None, "blk", None), P(), P("pair", None, "blk", None)),
        check_vma=False,
    )
```

profile of v0, /device:TPU:0, one launch (start us, length us, event | category | flops | bytes accessed | tf_op | source)
XLA Modules:
  0.0 494.4 jit_solution(1043420342084576107)
XLA Ops:
  8.6 129.2 %all-gather.3.cloned.1.call-done = bf16[1,64,256,256]{3,2,1,0:T(8,128)(2,1)} async-done(((bf16[1,64,32,256]{3,2,1,0:T(8,128)(2,1)}), bf16[1,64,256,256]{3,2,1,0:T(8,128)(2,1)}) %all-gather.3.cloned.1.call-update) | async-done | bytes 8388624 | tf_op jit(solution)/shard_map/all_gather | solution.py:174
  137.9 2.8 select_bitcast_fusion.1
  141.7 2.5 fusion.30
  146.6 4.5 collective-permute-start
  151.1 2.8 fusion.78
  155.8 2.7 fusion.76
  158.5 7.6 %concatenate.75 = bf16[64,32,820]{2,1,0:T(8,128)(2,1)} concatenate(bf16[64,32,164]{2,1,0:T(8,128)(2,1)} %get-tuple-element.86, bf16[64,32,164]{2,1,0:T(8,128)(2,1)} %get-tuple-element.87, bf16[64,32,128]{2,1,0:T(8,128)(2,1)S(1)} %bitcast.177, bf16[64,32,36]{2,1,0:T(8,128)(2,1)S(1)} %copy.20, bf16[64,32,164]{2,1,0:T(8,128)(2,1)S(1)} %get-tuple-element.56, ...), dimensions={2} | concatenate | bytes 6717440 | tf_op jit(solution)/shard_map/concatenate | solution.py:46
  166.1 4.4 fusion.34
  172.5 5.6 %collective-permute-start.2 = (bf16[64,2,128]{2,1,0:T(2,128)(2,1)}, bf16[64,2,128]{2,1,0:T(2,128)(2,1)}, u32[]{:S(2)}, u32[]{:S(2)}) collective-permute-start(bf16[64,2,128]{2,1,0:T(2,128)(2,1)} %get-tuple-element.78), channel_id=1, source_target_pairs={{0,1},{1,2},{2,3},{3,4},{4,5},{5,6},{6,7},{8,9},{9,10},{10,11},{11... | collective-permute-start | bytes 98312 | tf_op jit(solution)/shard_map/ppermute | solution.py:18
  201.7 7.6 %concatenate.90 = bf16[2048,820]{1,0:T(8,128)(2,1)} concatenate(bf16[2048,164]{1,0:T(8,128)(2,1)} %bitcast.185, bf16[2048,164]{1,0:T(8,128)(2,1)} %bitcast.186, bf16[2048,128]{1,0:T(8,128)(2,1)S(1)} %bitcast.178, bf16[2048,36]{1,0:T(8,128)(2,1)S(1)} %bitcast.173, bf16[2048,164]{1,0:T(8,128)(2,1)S(1)} %bitcast.184, bf16[2048,164]{1,0:T(8,128)(2,1)S(1)} %bitcast.183), dimensions={1} | concatenate | bytes 6717440 | tf_op jit(solution)/shard_map/concatenate | solution.py:46
  209.3 6.0 %copy.32 = bf16[820,2048]{1,0:T(8,128)(2,1)} copy(bf16[820,2048]{0,1:T(8,128)(2,1)} %bitcast.182) | data formatting | bytes 6717440 | tf_op jit(solution)/shard_map/dot_general | solution.py:73
  215.4 4.3 reshape.193
  221.2 2.8 fusion.75
  224.0 8.0 %concatenate.79 = bf16[64,32,820]{2,1,0:T(8,128)(2,1)} concatenate(bf16[64,32,164]{2,1,0:T(8,128)(2,1)} %get-tuple-element.54, bf16[64,32,164]{2,1,0:T(8,128)(2,1)} %get-tuple-element.53, bf16[64,32,164]{2,1,0:T(8,128)(2,1)} %get-tuple-element.52, bf16[64,32,164]{2,1,0:T(8,128)(2,1)S(1)} %get-tuple-element.51, bf16[64,32,164]{2,1,0:T(8,128)(2,1)S(1)} %get-tuple-element.50), dimensions={2} | concatenate | bytes 6717440 | tf_op jit(solution)/shard_map/concatenate | solution.py:46
  232.0 3.4 fusion.17
  239.0 2.4 pad_slice_fusion.3
  242.4 8.3 %concatenate.81 = bf16[64,32,820]{2,1,0:T(8,128)(2,1)} concatenate(bf16[64,32,164]{2,1,0:T(8,128)(2,1)} %get-tuple-element.73, bf16[64,32,164]{2,1,0:T(8,128)(2,1)} %get-tuple-element.71, bf16[64,32,128]{2,1,0:T(8,128)(2,1)} %copy-done.22, bf16[64,32,36]{2,1,0:T(8,128)(2,1)S(1)} %copy.20, bf16[64,32,164]{2,1,0:T(8,128)(2,1)} %get-tuple-element.72, ...), dimensions={2} | concatenate | bytes 6717440 | tf_op jit(solution)/shard_map/concatenate | solution.py:46
  250.6 4.5 fusion.16
  255.2 3.3 fusion.44
  261.1 8.5 %concatenate.83 = bf16[64,32,820]{2,1,0:T(8,128)(2,1)} concatenate(bf16[64,32,164]{2,1,0:T(8,128)(2,1)} %get-tuple-element.69, bf16[64,32,164]{2,1,0:T(8,128)(2,1)} %get-tuple-element.68, bf16[64,32,164]{2,1,0:T(8,128)(2,1)} %get-tuple-element.67, bf16[64,32,164]{2,1,0:T(8,128)(2,1)} %get-tuple-element.66, bf16[64,32,164]{2,1,0:T(8,128)(2,1)} %get-tuple-element.65), dimensions={2} | concatenate | bytes 6717440 | tf_op jit(solution)/shard_map/concatenate | solution.py:46
  269.7 5.3 %fusion.48 = (bf16[64,32,128]{2,1,0:T(8,128)(2,1)S(1)}, bf16[64,32,128]{2,1,0:T(8,128)(2,1)S(1)}, bf16[1,64,32,128]{3,2,1,0:T(8,128)(2,1)}) fusion(f32[64,32,128]{2,1,0:T(8,128)} %fusion.16, bf16[64,32,128]{2,1,0:T(8,128)(2,1)S(1)} %copy-done.23, f32[1,64,32,128]{3,2,1,0:T(8,128)} %param.14, bf16[1,3,64,32,128]{4,3,2,1,0:T(8,128)(2,1)} %param.12, ...), kind=kOutput, calls=%fused_computation.80 | convolution fusion | flops 434634752 | bytes 8287232 | tf_op jit(solution)/shard_map/dot_general | solution.py:59
  290.7 6.0 %copy.35 = bf16[820,2048]{1,0:T(8,128)(2,1)} copy(bf16[820,2048]{0,1:T(8,128)(2,1)} %bitcast.181) | data formatting | bytes 6717440 | tf_op jit(solution)/shard_map/dot_general | solution.py:73
  296.7 4.2 reshape.208
  300.8 6.0 %copy.34 = bf16[820,2048]{1,0:T(8,128)(2,1)} copy(bf16[820,2048]{0,1:T(8,128)(2,1)} %bitcast.180) | data formatting | bytes 6717440 | tf_op jit(solution)/shard_map/dot_general | solution.py:73
  306.8 4.4 reshape.204
  311.3 4.0 convolution_bitcast_fusion.1
  317.1 6.0 %copy.33 = bf16[820,2048]{1,0:T(8,128)(2,1)} copy(bf16[820,2048]{0,1:T(8,128)(2,1)} %bitcast.174) | data formatting | bytes 6717440 | tf_op jit(solution)/shard_map/dot_general | solution.py:73
  323.1 4.2 reshape.201
  328.6 4.5 collective-permute-start.4
  350.9 5.7 %collective-permute-start.6 = (f32[64,2,128]{2,1,0:T(2,128)S(1)}, f32[64,2,128]{2,1,0:T(2,128)S(1)}, u32[]{:S(2)}, u32[]{:S(2)}) collective-permute-start(f32[64,2,128]{2,1,0:T(2,128)S(1)} %add_add_fusion.2), channel_id=1, source_target_pairs={{0,1},{1,2},{2,3},{3,4},{4,5},{5,6},{6,7},{8,9},{9,10},{10,11},{11... | collective-permute-start | bytes 196616 | tf_op jit(solution)/shard_map/ppermute | solution.py:18
  360.4 122.4 %all-reduce.38.cloned.1.call-done = f32[2,3,5,164,128]{4,3,2,1,0:T(8,128)} async-done(((f32[2,3,5,164,128]{4,3,2,1,0:T(8,128)}), f32[2,3,5,164,128]{4,3,2,1,0:T(8,128)}) %all-reduce.38.cloned.1.call-update) | async-done | bytes 2519056 | tf_op jit(solution)/shard_map/psum | solution.py:216
  482.8 4.5 copy.36
  (201 shorter events, 79.9 us)
Async XLA Ops:
  7.2 133.5 %copy-start = (bf16[1,64,32,256]{3,2,1,0:T(8,128)(2,1)S(1)}, bf16[1,64,32,256]{3,2,1,0:T(8,128)(2,1)}, u32[]{:S(2)}) copy-start(bf16[1,64,32,256]{3,2,1,0:T(8,128)(2,1)} %param.8) | copy-start | bytes 3145732
  7.2 130.7 %all-gather.3.cloned.1.call-start = ((), (), s32[]{:S(2)}) async-start(), calls=%async_computation.1 | async-start | bytes 9437184 | tf_op jit(solution)/shard_map/all_gather | solution.py:174
  7.9 474.8 %all-reduce.38.cloned.1.call-start = ((), (), s32[]{:S(2)}) async-start(), calls=%async_computation | async-start | bytes 5160960 | tf_op jit(solution)/shard_map/psum | solution.py:216
  141.7 9.4 %copy-start.17 = (bf16[2,3,5,164,128]{4,0,3,2,1:T(2,128)(2,1)S(1)}, bf16[2,3,5,164,128]{4,0,3,2,1:T(2,128)(2,1)}, u32[]{:S(2)}) copy-start(bf16[2,3,5,164,128]{4,0,3,2,1:T(2,128)(2,1)} %param.13) | copy-start | bytes 3778564
  145.3 9.6 %collective-permute-start.1 = (bf16[64,2,164]{2,1,0:T(2,128)(2,1)S(1)}, bf16[64,2,164]{2,1,0:T(2,128)(2,1)S(1)}, u32[]{:S(2)}, u32[]{:S(2)}) collective-permute-start(bf16[64,2,164]{2,1,0:T(2,128)(2,1)S(1)} %get-tuple-element.76), channel_id=1, source_target_pairs={{1,0},{2,1},{3,2},{4,3},{5,4},{6,5},{7,6},{9,8},{10,9},{11,10},{12... | collective-permute-start | bytes 125960 | tf_op jit(solution)/shard_map/ppermute | solution.py:21
  146.6 8.3 %collective-permute-start = (bf16[64,2,164]{2,1,0:T(2,128)(2,1)S(1)}, bf16[64,2,164]{2,1,0:T(2,128)(2,1)S(1)}, u32[]{:S(2)}, u32[]{:S(2)}) collective-permute-start(bf16[64,2,164]{2,1,0:T(2,128)(2,1)S(1)} %get-tuple-element.77), channel_id=1, source_target_pairs={{0,1},{1,2},{2,3},{3,4},{4,5},{5,6},{6,7},{8,9},{9,10},{10,11},{11... | collective-permute-start | bytes 125960 | tf_op jit(solution)/shard_map/ppermute | solution.py:18
  166.1 12.1 %copy-start.34 = (bf16[1,1,5,164,128]{4,0,3,2,1:T(2,128)(2,1)S(1)}, bf16[1,1,5,164,128]{4,0,3,2,1:T(2,128)(2,1)}, u32[]{:S(2)}) copy-start(bf16[1,1,5,164,128]{4,0,3,2,1:T(2,128)(2,1)} %get-tuple-element.59) | copy-start | bytes 629764
  166.1 12.8 %copy-start.33 = (bf16[1,1,5,164,128]{4,0,3,2,1:T(2,128)(2,1)S(1)}, bf16[1,1,5,164,128]{4,0,3,2,1:T(2,128)(2,1)}, u32[]{:S(2)}) copy-start(bf16[1,1,5,164,128]{4,0,3,2,1:T(2,128)(2,1)} %get-tuple-element.60) | copy-start | bytes 629764
  170.6 12.0 %copy-start.46 = (bf16[64,32,128]{2,1,0:T(8,128)(2,1)}, bf16[64,32,128]{2,1,0:T(8,128)(2,1)S(1)}, u32[]{:S(2)}) copy-start(bf16[64,32,128]{2,1,0:T(8,128)(2,1)S(1)} %get-tuple-element.80) | copy-start | bytes 1572868
  170.6 9.8 %copy-start.32 = (bf16[1,1,5,164,128]{4,0,3,2,1:T(2,128)(2,1)S(1)}, bf16[1,1,5,164,128]{4,0,3,2,1:T(2,128)(2,1)}, u32[]{:S(2)}) copy-start(bf16[1,1,5,164,128]{4,0,3,2,1:T(2,128)(2,1)} %get-tuple-element.61) | copy-start | bytes 629764
  170.6 11.2 %copy-start.31 = (bf16[1,1,5,164,128]{4,0,3,2,1:T(2,128)(2,1)S(1)}, bf16[1,1,5,164,128]{4,0,3,2,1:T(2,128)(2,1)}, u32[]{:S(2)}) copy-start(bf16[1,1,5,164,128]{4,0,3,2,1:T(2,128)(2,1)} %get-tuple-element.62) | copy-start | bytes 629764
  171.2 48.4 %collective-permute-start.3 = (bf16[64,2,128]{2,1,0:T(2,128)(2,1)}, bf16[64,2,128]{2,1,0:T(2,128)(2,1)S(1)}, u32[]{:S(2)}, u32[]{:S(2)}) collective-permute-start(bf16[64,2,128]{2,1,0:T(2,128)(2,1)} %get-tuple-element.79), channel_id=1, source_target_pairs={{1,0},{2,1},{3,2},{4,3},{5,4},{6,5},{7,6},{9,8},{10,9},{11,10},{12... | collective-permute-start | bytes 98312 | tf_op jit(solution)/shard_map/ppermute | solution.py:21
  172.5 47.1 %collective-permute-start.2 = (bf16[64,2,128]{2,1,0:T(2,128)(2,1)}, bf16[64,2,128]{2,1,0:T(2,128)(2,1)}, u32[]{:S(2)}, u32[]{:S(2)}) collective-permute-start(bf16[64,2,128]{2,1,0:T(2,128)(2,1)} %get-tuple-element.78), channel_id=1, source_target_pairs={{0,1},{1,2},{2,3},{3,4},{4,5},{5,6},{6,7},{8,9},{9,10},{10,11},{11... | collective-permute-start | bytes 98312 | tf_op jit(solution)/shard_map/ppermute | solution.py:18
  178.2 5.0 %copy-start.30 = (bf16[1,1,5,164,128]{4,0,3,2,1:T(2,128)(2,1)S(1)}, bf16[1,1,5,164,128]{4,0,3,2,1:T(2,128)(2,1)}, u32[]{:S(2)}) copy-start(bf16[1,1,5,164,128]{4,0,3,2,1:T(2,128)(2,1)} %copy-done.29) | copy-start | bytes 629764
  179.0 5.0 %copy-start.28 = (bf16[1,1,5,164,128]{4,0,3,2,1:T(2,128)(2,1)S(1)}, bf16[1,1,5,164,128]{4,0,3,2,1:T(2,128)(2,1)}, u32[]{:S(2)}) copy-start(bf16[1,1,5,164,128]{4,0,3,2,1:T(2,128)(2,1)} %get-tuple-element.64) | copy-start | bytes 629764
  224.0 8.0 %copy-start.45 = (bf16[820,128,1]{1,0,2:T(8,128)(2,1)S(1)}, bf16[820,128,1]{1,0,2:T(8,128)(2,1)}, u32[]{:S(2)}) copy-start(bf16[820,128,1]{1,0,2:T(8,128)(2,1)} %reshape.226) | copy-start | bytes 629764
  237.9 47.4 %copy-start.11 = (f32[64,32,128]{2,1,0:T(8,128)}, f32[64,32,128]{2,1,0:T(8,128)S(1)}, u32[]{:S(2)}) copy-start(f32[64,32,128]{2,1,0:T(8,128)S(1)} %get-tuple-element.83) | copy-start | bytes 3145732
  250.6 4.5 copy-start.8
  250.6 4.5 copy-start.23
  250.6 4.5 copy-start.58
  269.7 6.1 %copy-start.52 = (bf16[5,128,128]{2,1,0:T(8,128)(2,1)S(1)}, bf16[5,128,128]{2,1,0:T(8,128)(2,1)}, u32[]{:S(2)}) copy-start(bf16[5,128,128]{2,1,0:T(8,128)(2,1)} %slice.398) | copy-start | bytes 491524
  275.0 5.6 %copy-start.39 = (bf16[64,32,128]{2,1,0:T(8,128)(2,1)}, bf16[64,32,128]{2,1,0:T(8,128)(2,1)S(1)}, u32[]{:S(2)}) copy-start(bf16[64,32,128]{2,1,0:T(8,128)(2,1)S(1)} %get-tuple-element.47) | copy-start | bytes 1572868
  323.1 10.1 %copy-start.48 = (bf16[5,128,128]{2,1,0:T(8,128)(2,1)S(1)}, bf16[5,128,128]{2,1,0:T(8,128)(2,1)}, u32[]{:S(2)}) copy-start(bf16[5,128,128]{2,1,0:T(8,128)(2,1)} %slice.423) | copy-start | bytes 491524
  327.3 14.4 %collective-permute-start.5 = (f32[64,2,128]{2,1,0:T(2,128)}, f32[64,2,128]{2,1,0:T(2,128)S(1)}, u32[]{:S(2)}, u32[]{:S(2)}) collective-permute-start(f32[64,2,128]{2,1,0:T(2,128)} %get-tuple-element.26), channel_id=1, source_target_pairs={{1,0},{2,1},{3,2},{4,3},{5,4},{6,5},{7,6},{9,8},{10,9},{11,10},{12... | collective-permute-start | bytes 196616 | tf_op jit(solution)/shard_map/ppermute | solution.py:21
  328.6 13.1 %collective-permute-start.4 = (f32[64,2,128]{2,1,0:T(2,128)S(1)}, f32[64,2,128]{2,1,0:T(2,128)S(1)}, u32[]{:S(2)}, u32[]{:S(2)}) collective-permute-start(f32[64,2,128]{2,1,0:T(2,128)S(1)} %get-tuple-element.25), channel_id=1, source_target_pairs={{0,1},{1,2},{2,3},{3,4},{4,5},{5,6},{6,7},{8,9},{9,10},{10,11},{11... | collective-permute-start | bytes 196616 | tf_op jit(solution)/shard_map/ppermute | solution.py:18
  349.4 9.0 %collective-permute-start.7 = (f32[64,2,128]{2,1,0:T(2,128)S(1)}, f32[64,2,128]{2,1,0:T(2,128)S(1)}, u32[]{:S(2)}, u32[]{:S(2)}) collective-permute-start(f32[64,2,128]{2,1,0:T(2,128)S(1)} %add_add_fusion.1), channel_id=1, source_target_pairs={{1,0},{2,1},{3,2},{4,3},{5,4},{6,5},{7,6},{9,8},{10,9},{11,10},{12... | collective-permute-start | bytes 196616 | tf_op jit(solution)/shard_map/ppermute | solution.py:21
  350.8 8.0 %copy-start.12 = (f32[64,32,128]{2,1,0:T(8,128)S(1)}, f32[64,32,128]{2,1,0:T(8,128)}, u32[]{:S(2)}) copy-start(f32[64,32,128]{2,1,0:T(8,128)} %copy-done.11) | copy-start | bytes 3145732
  350.9 8.0 %copy-start.14 = (f32[64,32,128]{2,1,0:T(8,128)S(1)}, f32[64,32,128]{2,1,0:T(8,128)}, u32[]{:S(2)}) copy-start(f32[64,32,128]{2,1,0:T(8,128)} %copy-done.13) | copy-start | bytes 3145732
  350.9 7.9 %copy-start.16 = (f32[64,36,128]{2,1,0:T(8,128)S(1)}, f32[64,36,128]{2,1,0:T(8,128)}, u32[]{:S(2)}) copy-start(f32[64,36,128]{2,1,0:T(8,128)} %pad_add_fusion) | copy-start | bytes 3538948
  350.9 7.9 %copy-start.26 = (f32[64,32,128]{2,1,0:T(8,128)S(1)}, f32[64,32,128]{2,1,0:T(8,128)}, u32[]{:S(2)}) copy-start(f32[64,32,128]{2,1,0:T(8,128)} %get-tuple-element.81) | copy-start | bytes 3145732
  350.9 7.9 %collective-permute-start.6 = (f32[64,2,128]{2,1,0:T(2,128)S(1)}, f32[64,2,128]{2,1,0:T(2,128)S(1)}, u32[]{:S(2)}, u32[]{:S(2)}) collective-permute-start(f32[64,2,128]{2,1,0:T(2,128)S(1)} %add_add_fusion.2), channel_id=1, source_target_pairs={{0,1},{1,2},{2,3},{3,4},{4,5},{5,6},{6,7},{8,9},{9,10},{10,11},{11... | collective-permute-start | bytes 196616 | tf_op jit(solution)/shard_map/ppermute | solution.py:18
  358.8 128.4 %copy-start.1 = (bf16[1,64,32,256]{3,2,1,0:T(8,128)(2,1)S(1)}, bf16[1,64,32,256]{3,2,1,0:T(8,128)(2,1)}, u32[]{:S(2)}) copy-start(bf16[1,64,32,256]{3,2,1,0:T(8,128)(2,1)} %param.8) | copy-start | bytes 3145732
  (38 other events, 80.8 us)
Sparse Core Ops, SparseCore 0:
  10.2 127.6 all-gather.2
  346.7 136.0 all-reduce.37
where the time goes:
time: 504 us; the launch traced here: 494 us
  waiting for transfers between devices  253 us (50%)
  local copies, waits for them, and re-layouts  141 us (28%)
  matrix products  41.8 us (8%)
  starting transfers between devices  25.7 us (5%)
  other arithmetic  17.8 us (4%)
  between operations  15.8 us (3%)
    all_gather x1, waiting for transfers between devices, on_device(): shards = lax.all_gather(right_block, 'blk', axis=1, tiled=True)  129 us
    psum x1, waiting for transfers between devices, on_device(): lax.psum(jnp.stack([first_grads, second_grads]), ('pair', 'blk'))  122 us
    concatenate x5, local copies, waits for them, and re-layouts, tap_stack(): jnp.concatenate([lax.slice_in_dim(padded, tap_id, tap_id + extent, axis=a...  40 us
    dot_general x4, local copies, waits for them, and re-layouts, conv_weight_grad(): lax.dot_general(flat_taps, flat_deltas, (((0,), (0,)), ((), ())), preferr...  24 us
    dot_general x6, matrix products, conv_apply(): jnp.dot(flat_taps, weight_taps.reshape(kernel_len * in_chan, out_chan), p...  23.4 us
    unnamed x133, local copies, waits for them, and re-layouts  22.1 us
    ppermute x4, starting transfers between devices, with_halo(): lax.ppermute(lax.slice_in_dim(block, block.shape[dim] - width, None, axis...  20.5 us
    another operation x4, local copies, waits for them, and re-layouts  17 us
  transfers between devices with their start and end apart: 10, of which 3 were waited for; matrix products, arithmetic and copies ran while one was open for 11% of the time, Pallas kernels for 0%

commit v1 on v0

--- a/solution.py
+++ b/solution.py
@@ -213,7 +213,7 @@
     first_grads, hidden_back = section_backward(
         first_back, first_stored, gru_weights[0], 1, stripe_rims
     )
-    grad_stack = lax.psum(jnp.stack([first_grads, second_grads]), ("pair", "blk"))
+    grad_stack = lax.psum(lax.psum(jnp.stack([first_grads, second_grads]), "blk"), "pair")
     return (second_new.astype(jnp.bfloat16)[None], grad_stack, hidden_back[None])
 
 

time: 504 us -> 537 us (1.065)
  waiting for transfers between devices: 253 us -> 289 us
    psum x1 -> x2, waiting for transfers between devices: 122 us -> 159 us  [the longest x1 111 us: on_device(): lax.psum(jnp.stack([first_grads, second_grads]), 'blk')]
    unnamed x133 -> x125, local copies, waits for them, and re-layouts: 22.1 us -> 20.6 us
  transfers between devices with their start and end apart: 10 -> 11, of which waited for: 3 -> 3; matrix products, arithmetic and copies ran while one was open for 11% -> 10% of each run, Pallas kernels for 0% -> 0%
where the time goes in v1:
time: 537 us; the launch traced here: 527 us
  waiting for transfers between devices  289 us (54%)
  local copies, waits for them, and re-layouts  137 us (26%)
  matrix products  44 us (8%)
  starting transfers between devices  25.3 us (5%)
  other arithmetic  16.7 us (3%)
  between operations  15.6 us (3%)
    all_gather x1, waiting for transfers between devices, on_device(): shards = lax.all_gather(right_block, 'blk', axis=1, tiled=True)  129 us
    psum x1, waiting for transfers between devices, on_device(): lax.psum(jnp.stack([first_grads, second_grads]), 'blk')  111 us
    psum x1, waiting for transfers between devices, on_device(): lax.psum(lax.psum(jnp.stack([first_grads, second_grads]), 'blk'), 'pair')  47.3 us
    concatenate x5, local copies, waits for them, and re-layouts, tap_stack(): jnp.concatenate([lax.slice_in_dim(padded, tap_id, tap_id + extent, axis=a...  40 us
    dot_general x4, local copies, waits for them, and re-layouts, conv_weight_grad(): lax.dot_general(flat_taps, flat_deltas, (((0,), (0,)), ((), ())), preferr...  24.6 us
    dot_general x6, matrix products, conv_apply(): jnp.dot(flat_taps, weight_taps.reshape(kernel_len * in_chan, out_chan), p...  23.4 us
    unnamed x125, local copies, waits for them, and re-layouts  20.6 us
    ppermute x4, starting transfers between devices, with_halo(): lax.ppermute(lax.slice_in_dim(block, block.shape[dim] - width, None, axis...  19.8 us
  transfers between devices with their start and end apart: 11, of which 3 were waited for; matrix products, arithmetic and copies ran while one was open for 10% of the time, Pallas kernels for 0%

profile of v1, /device:TPU:0, one launch (start us, length us, event | category | flops | bytes accessed | tf_op | source)
XLA Modules:
  0.0 526.7 jit_solution(5640864698744101994)
XLA Ops:
  8.6 129.2 %all-gather.3.cloned.1.call-done = bf16[1,64,256,256]{3,2,1,0:T(8,128)(2,1)} async-done(((bf16[1,64,32,256]{3,2,1,0:T(8,128)(2,1)}), bf16[1,64,256,256]{3,2,1,0:T(8,128)(2,1)}) %all-gather.3.cloned.1.call-update) | async-done | bytes 8388624 | tf_op jit(solution)/shard_map/all_gather | solution.py:174
  137.9 2.8 select_bitcast_fusion.1
  146.6 4.5 collective-permute-start
  151.1 2.9 fusion.78
  155.8 2.7 fusion.76
  158.5 7.6 %concatenate.75 = bf16[64,32,820]{2,1,0:T(8,128)(2,1)} concatenate(bf16[64,32,164]{2,1,0:T(8,128)(2,1)} %get-tuple-element.86, bf16[64,32,164]{2,1,0:T(8,128)(2,1)} %get-tuple-element.87, bf16[64,32,128]{2,1,0:T(8,128)(2,1)S(1)} %bitcast.177, bf16[64,32,36]{2,1,0:T(8,128)(2,1)S(1)} %copy.20, bf16[64,32,164]{2,1,0:T(8,128)(2,1)S(1)} %get-tuple-element.56, ...), dimensions={2} | concatenate | bytes 6717440 | tf_op jit(solution)/shard_map/concatenate | solution.py:46
  166.2 4.4 fusion.34
  172.6 5.6 %collective-permute-start.2 = (bf16[64,2,128]{2,1,0:T(2,128)(2,1)}, bf16[64,2,128]{2,1,0:T(2,128)(2,1)}, u32[]{:S(2)}, u32[]{:S(2)}) collective-permute-start(bf16[64,2,128]{2,1,0:T(2,128)(2,1)} %get-tuple-element.78), channel_id=1, source_target_pairs={{0,1},{1,2},{2,3},{3,4},{4,5},{5,6},{6,7},{8,9},{9,10},{10,11},{11... | collective-permute-start | bytes 98312 | tf_op jit(solution)/shard_map/ppermute | solution.py:18
  198.0 7.6 %concatenate.90 = bf16[2048,820]{1,0:T(8,128)(2,1)} concatenate(bf16[2048,164]{1,0:T(8,128)(2,1)} %bitcast.185, bf16[2048,164]{1,0:T(8,128)(2,1)} %bitcast.186, bf16[2048,128]{1,0:T(8,128)(2,1)S(1)} %bitcast.178, bf16[2048,36]{1,0:T(8,128)(2,1)S(1)} %bitcast.173, bf16[2048,164]{1,0:T(8,128)(2,1)S(1)} %bitcast.184, bf16[2048,164]{1,0:T(8,128)(2,1)S(1)} %bitcast.183), dimensions={1} | concatenate | bytes 6717440 | tf_op jit(solution)/shard_map/concatenate | solution.py:46
  205.6 6.1 %copy.32 = bf16[820,2048]{1,0:T(8,128)(2,1)} copy(bf16[820,2048]{0,1:T(8,128)(2,1)} %bitcast.182) | data formatting | bytes 6717440 | tf_op jit(solution)/shard_map/dot_general | solution.py:73
  211.7 4.2 reshape.193
  217.5 2.8 fusion.75
  220.3 7.9 %concatenate.79 = bf16[64,32,820]{2,1,0:T(8,128)(2,1)} concatenate(bf16[64,32,164]{2,1,0:T(8,128)(2,1)} %get-tuple-element.54, bf16[64,32,164]{2,1,0:T(8,128)(2,1)} %get-tuple-element.53, bf16[64,32,164]{2,1,0:T(8,128)(2,1)} %get-tuple-element.52, bf16[64,32,164]{2,1,0:T(8,128)(2,1)S(1)} %get-tuple-element.51, bf16[64,32,164]{2,1,0:T(8,128)(2,1)S(1)} %get-tuple-element.50), dimensions={2} | concatenate | bytes 6717440 | tf_op jit(solution)/shard_map/concatenate | solution.py:46
  228.3 3.4 fusion.17
  238.6 8.3 %concatenate.81 = bf16[64,32,820]{2,1,0:T(8,128)(2,1)} concatenate(bf16[64,32,164]{2,1,0:T(8,128)(2,1)} %get-tuple-element.73, bf16[64,32,164]{2,1,0:T(8,128)(2,1)} %get-tuple-element.71, bf16[64,32,128]{2,1,0:T(8,128)(2,1)} %copy-done.21, bf16[64,32,36]{2,1,0:T(8,128)(2,1)S(1)} %copy.20, bf16[64,32,164]{2,1,0:T(8,128)(2,1)} %get-tuple-element.72, ...), dimensions={2} | concatenate | bytes 6717440 | tf_op jit(solution)/shard_map/concatenate | solution.py:46
  246.9 4.5 fusion.16
  251.4 3.3 fusion.44
  257.4 8.5 %concatenate.83 = bf16[64,32,820]{2,1,0:T(8,128)(2,1)} concatenate(bf16[64,32,164]{2,1,0:T(8,128)(2,1)} %get-tuple-element.69, bf16[64,32,164]{2,1,0:T(8,128)(2,1)} %get-tuple-element.68, bf16[64,32,164]{2,1,0:T(8,128)(2,1)} %get-tuple-element.67, bf16[64,32,164]{2,1,0:T(8,128)(2,1)} %get-tuple-element.66, bf16[64,32,164]{2,1,0:T(8,128)(2,1)} %get-tuple-element.65), dimensions={2} | concatenate | bytes 6717440 | tf_op jit(solution)/shard_map/concatenate | solution.py:46
  265.9 5.3 %fusion.48 = (bf16[64,32,128]{2,1,0:T(8,128)(2,1)S(1)}, bf16[64,32,128]{2,1,0:T(8,128)(2,1)S(1)}, bf16[1,64,32,128]{3,2,1,0:T(8,128)(2,1)}) fusion(f32[64,32,128]{2,1,0:T(8,128)} %fusion.16, bf16[64,32,128]{2,1,0:T(8,128)(2,1)S(1)} %copy-done.22, f32[1,64,32,128]{3,2,1,0:T(8,128)} %param.14, bf16[1,3,64,32,128]{4,3,2,1,0:T(8,128)(2,1)} %param.12, ...), kind=kOutput, calls=%fused_computation.80 | convolution fusion | flops 434634752 | bytes 8287232 | tf_op jit(solution)/shard_map/dot_general | solution.py:59
  285.8 6.5 %copy.35 = bf16[820,2048]{1,0:T(8,128)(2,1)} copy(bf16[820,2048]{0,1:T(8,128)(2,1)} %bitcast.181) | data formatting | bytes 6717440 | tf_op jit(solution)/shard_map/dot_general | solution.py:73
  292.3 4.2 reshape.208
  296.5 6.0 %copy.34 = bf16[820,2048]{1,0:T(8,128)(2,1)} copy(bf16[820,2048]{0,1:T(8,128)(2,1)} %bitcast.180) | data formatting | bytes 6717440 | tf_op jit(solution)/shard_map/dot_general | solution.py:73
  302.5 4.5 reshape.204
  307.0 3.2 convolution_bitcast_fusion.1
  312.0 6.0 %copy.33 = bf16[820,2048]{1,0:T(8,128)(2,1)} copy(bf16[820,2048]{0,1:T(8,128)(2,1)} %bitcast.174) | data formatting | bytes 6717440 | tf_op jit(solution)/shard_map/dot_general | solution.py:73
  318.0 4.2 reshape.201
  323.8 4.5 collective-permute-start.4
  328.4 3.0 convolution_bitcast_fusion
  343.2 111.4 %all-reduce.39.cloned.1.call-done = f32[2,3,5,164,128]{4,3,2,1,0:T(8,128)} async-done(((f32[2,3,5,164,128]{4,3,2,1,0:T(8,128)}), f32[2,3,5,164,128]{4,3,2,1,0:T(8,128)}) %all-reduce.39.cloned.1.call-update) | async-done | bytes 2519056 | tf_op jit(solution)/shard_map/psum | solution.py:216
  459.7 5.1 collective-permute-start.6
  468.1 47.3 %all-reduce.41.cloned.1.call-done = f32[2,3,5,164,128]{4,3,2,1,0:T(8,128)} async-done(((f32[2,3,5,164,128]{4,3,2,1,0:T(8,128)}), f32[2,3,5,164,128]{4,3,2,1,0:T(8,128)}) %all-reduce.41.cloned.1.call-update) | async-done | bytes 2519056 | tf_op jit(solution)/shard_map/psum | solution.py:216
  515.4 4.5 copy.36
  (196 shorter events, 79.0 us)
Async XLA Ops:
  7.2 133.5 %copy-start = (bf16[1,64,32,256]{3,2,1,0:T(8,128)(2,1)S(1)}, bf16[1,64,32,256]{3,2,1,0:T(8,128)(2,1)}, u32[]{:S(2)}) copy-start(bf16[1,64,32,256]{3,2,1,0:T(8,128)(2,1)} %param.8) | copy-start | bytes 3145732
  7.2 130.7 %all-gather.3.cloned.1.call-start = ((), (), s32[]{:S(2)}) async-start(), calls=%async_computation.2 | async-start | bytes 9437184 | tf_op jit(solution)/shard_map/all_gather | solution.py:174
  7.9 446.7 %all-reduce.39.cloned.1.call-start = ((), (), s32[]{:S(2)}) async-start(), calls=%async_computation | async-start | bytes 5160960 | tf_op jit(solution)/shard_map/psum | solution.py:216
  141.7 9.4 %copy-start.15 = (bf16[2,3,5,164,128]{4,0,3,2,1:T(2,128)(2,1)S(1)}, bf16[2,3,5,164,128]{4,0,3,2,1:T(2,128)(2,1)}, u32[]{:S(2)}) copy-start(bf16[2,3,5,164,128]{4,0,3,2,1:T(2,128)(2,1)} %param.13) | copy-start | bytes 3778564
  145.3 9.6 %collective-permute-start.1 = (bf16[64,2,164]{2,1,0:T(2,128)(2,1)S(1)}, bf16[64,2,164]{2,1,0:T(2,128)(2,1)S(1)}, u32[]{:S(2)}, u32[]{:S(2)}) collective-permute-start(bf16[64,2,164]{2,1,0:T(2,128)(2,1)S(1)} %get-tuple-element.76), channel_id=1, source_target_pairs={{1,0},{2,1},{3,2},{4,3},{5,4},{6,5},{7,6},{9,8},{10,9},{11,10},{12... | collective-permute-start | bytes 125960 | tf_op jit(solution)/shard_map/ppermute | solution.py:21
  146.6 8.3 %collective-permute-start = (bf16[64,2,164]{2,1,0:T(2,128)(2,1)S(1)}, bf16[64,2,164]{2,1,0:T(2,128)(2,1)S(1)}, u32[]{:S(2)}, u32[]{:S(2)}) collective-permute-start(bf16[64,2,164]{2,1,0:T(2,128)(2,1)S(1)} %get-tuple-element.77), channel_id=1, source_target_pairs={{0,1},{1,2},{2,3},{3,4},{4,5},{5,6},{6,7},{8,9},{9,10},{10,11},{11... | collective-permute-start | bytes 125960 | tf_op jit(solution)/shard_map/ppermute | solution.py:18
  166.2 12.1 %copy-start.33 = (bf16[1,1,5,164,128]{4,0,3,2,1:T(2,128)(2,1)S(1)}, bf16[1,1,5,164,128]{4,0,3,2,1:T(2,128)(2,1)}, u32[]{:S(2)}) copy-start(bf16[1,1,5,164,128]{4,0,3,2,1:T(2,128)(2,1)} %get-tuple-element.59) | copy-start | bytes 629764
  166.2 12.8 %copy-start.32 = (bf16[1,1,5,164,128]{4,0,3,2,1:T(2,128)(2,1)S(1)}, bf16[1,1,5,164,128]{4,0,3,2,1:T(2,128)(2,1)}, u32[]{:S(2)}) copy-start(bf16[1,1,5,164,128]{4,0,3,2,1:T(2,128)(2,1)} %get-tuple-element.60) | copy-start | bytes 629764
  170.6 11.9 %copy-start.44 = (bf16[64,32,128]{2,1,0:T(8,128)(2,1)}, bf16[64,32,128]{2,1,0:T(8,128)(2,1)S(1)}, u32[]{:S(2)}) copy-start(bf16[64,32,128]{2,1,0:T(8,128)(2,1)S(1)} %get-tuple-element.80) | copy-start | bytes 1572868
  170.6 9.8 %copy-start.31 = (bf16[1,1,5,164,128]{4,0,3,2,1:T(2,128)(2,1)S(1)}, bf16[1,1,5,164,128]{4,0,3,2,1:T(2,128)(2,1)}, u32[]{:S(2)}) copy-start(bf16[1,1,5,164,128]{4,0,3,2,1:T(2,128)(2,1)} %get-tuple-element.61) | copy-start | bytes 629764
  170.6 11.2 %copy-start.30 = (bf16[1,1,5,164,128]{4,0,3,2,1:T(2,128)(2,1)S(1)}, bf16[1,1,5,164,128]{4,0,3,2,1:T(2,128)(2,1)}, u32[]{:S(2)}) copy-start(bf16[1,1,5,164,128]{4,0,3,2,1:T(2,128)(2,1)} %get-tuple-element.62) | copy-start | bytes 629764
  171.3 44.6 %collective-permute-start.3 = (bf16[64,2,128]{2,1,0:T(2,128)(2,1)}, bf16[64,2,128]{2,1,0:T(2,128)(2,1)S(1)}, u32[]{:S(2)}, u32[]{:S(2)}) collective-permute-start(bf16[64,2,128]{2,1,0:T(2,128)(2,1)} %get-tuple-element.79), channel_id=1, source_target_pairs={{1,0},{2,1},{3,2},{4,3},{5,4},{6,5},{7,6},{9,8},{10,9},{11,10},{12... | collective-permute-start | bytes 98312 | tf_op jit(solution)/shard_map/ppermute | solution.py:21
  172.6 43.4 %collective-permute-start.2 = (bf16[64,2,128]{2,1,0:T(2,128)(2,1)}, bf16[64,2,128]{2,1,0:T(2,128)(2,1)}, u32[]{:S(2)}, u32[]{:S(2)}) collective-permute-start(bf16[64,2,128]{2,1,0:T(2,128)(2,1)} %get-tuple-element.78), channel_id=1, source_target_pairs={{0,1},{1,2},{2,3},{3,4},{4,5},{5,6},{6,7},{8,9},{9,10},{10,11},{11... | collective-permute-start | bytes 98312 | tf_op jit(solution)/shard_map/ppermute | solution.py:18
  220.3 8.0 %copy-start.43 = (bf16[820,128,1]{1,0,2:T(8,128)(2,1)S(1)}, bf16[820,128,1]{1,0,2:T(8,128)(2,1)}, u32[]{:S(2)}) copy-start(bf16[820,128,1]{1,0,2:T(8,128)(2,1)} %reshape.226) | copy-start | bytes 629764
  234.1 47.4 %copy-start.9 = (f32[64,32,128]{2,1,0:T(8,128)}, f32[64,32,128]{2,1,0:T(8,128)S(1)}, u32[]{:S(2)}) copy-start(f32[64,32,128]{2,1,0:T(8,128)S(1)} %get-tuple-element.83) | copy-start | bytes 3145732
  246.9 4.5 copy-start.54
  265.9 6.1 %copy-start.48 = (bf16[5,128,128]{2,1,0:T(8,128)(2,1)S(1)}, bf16[5,128,128]{2,1,0:T(8,128)(2,1)}, u32[]{:S(2)}) copy-start(bf16[5,128,128]{2,1,0:T(8,128)(2,1)} %slice.398) | copy-start | bytes 491524
  271.2 5.5 %copy-start.38 = (bf16[64,32,128]{2,1,0:T(8,128)(2,1)}, bf16[64,32,128]{2,1,0:T(8,128)(2,1)S(1)}, u32[]{:S(2)}) copy-start(bf16[64,32,128]{2,1,0:T(8,128)(2,1)S(1)} %get-tuple-element.47) | copy-start | bytes 1572868
  285.8 48.8 %copy-start.13 = (f32[64,36,128]{2,1,0:T(8,128)}, f32[64,36,128]{2,1,0:T(8,128)S(1)}, u32[]{:S(2)}) copy-start(f32[64,36,128]{2,1,0:T(8,128)S(1)} %pad_add_fusion) | copy-start | bytes 3538948
  318.0 10.3 %copy-start.37 = (bf16[64,32,128]{2,1,0:T(8,128)(2,1)S(1)}, bf16[64,32,128]{2,1,0:T(8,128)(2,1)}, u32[]{:S(2)}) copy-start(bf16[64,32,128]{2,1,0:T(8,128)(2,1)} %copy-done.36) | copy-start | bytes 1572868
  322.2 9.2 %copy-start.8 = (bf16[5,164,2048]{2,1,0:T(8,128)(2,1)S(1)}, bf16[5,164,2048]{2,1,0:T(8,128)(2,1)}, u32[]{:S(2)}) copy-start(bf16[5,164,2048]{2,1,0:T(8,128)(2,1)} %reshape.201) | copy-start | bytes 10076164
  322.3 9.2 %copy-start.19 = (bf16[64,32,128]{2,1,0:T(8,128)(2,1)S(1)}, bf16[64,32,128]{2,1,0:T(8,128)(2,1)}, u32[]{:S(2)}) copy-start(bf16[64,32,128]{2,1,0:T(8,128)(2,1)} %copy-done.18) | copy-start | bytes 1572868
  322.3 12.4 %collective-permute-start.5 = (f32[64,2,128]{2,1,0:T(2,128)}, f32[64,2,128]{2,1,0:T(2,128)S(1)}, u32[]{:S(2)}, u32[]{:S(2)}) collective-permute-start(f32[64,2,128]{2,1,0:T(2,128)} %get-tuple-element.26), channel_id=1, source_target_pairs={{1,0},{2,1},{3,2},{4,3},{5,4},{6,5},{7,6},{9,8},{10,9},{11,10},{12... | collective-permute-start | bytes 196616 | tf_op jit(solution)/shard_map/ppermute | solution.py:21
  323.8 10.8 %collective-permute-start.4 = (f32[64,2,128]{2,1,0:T(2,128)S(1)}, f32[64,2,128]{2,1,0:T(2,128)S(1)}, u32[]{:S(2)}, u32[]{:S(2)}) collective-permute-start(f32[64,2,128]{2,1,0:T(2,128)S(1)} %get-tuple-element.25), channel_id=1, source_target_pairs={{0,1},{1,2},{2,3},{3,4},{4,5},{5,6},{6,7},{8,9},{9,10},{10,11},{11... | collective-permute-start | bytes 196616 | tf_op jit(solution)/shard_map/ppermute | solution.py:18
  339.2 176.3 %all-reduce.41.cloned.1.call-start = ((), (), s32[]{:S(2)}) async-start(), calls=%async_computation.1 | async-start | bytes 5160960 | tf_op jit(solution)/shard_map/psum | solution.py:216
  458.2 8.3 %collective-permute-start.7 = (f32[64,2,128]{2,1,0:T(2,128)S(1)}, f32[64,2,128]{2,1,0:T(2,128)S(1)}, u32[]{:S(2)}, u32[]{:S(2)}) collective-permute-start(f32[64,2,128]{2,1,0:T(2,128)S(1)} %add_add_fusion.1), channel_id=1, source_target_pairs={{1,0},{2,1},{3,2},{4,3},{5,4},{6,5},{7,6},{9,8},{10,9},{11,10},{12... | collective-permute-start | bytes 196616 | tf_op jit(solution)/shard_map/ppermute | solution.py:21
  459.7 6.9 %copy-start.10 = (f32[64,32,128]{2,1,0:T(8,128)S(1)}, f32[64,32,128]{2,1,0:T(8,128)}, u32[]{:S(2)}) copy-start(f32[64,32,128]{2,1,0:T(8,128)} %copy-done.9) | copy-start | bytes 3145732
  459.7 6.9 %copy-start.12 = (f32[64,32,128]{2,1,0:T(8,128)S(1)}, f32[64,32,128]{2,1,0:T(8,128)}, u32[]{:S(2)}) copy-start(f32[64,32,128]{2,1,0:T(8,128)} %copy-done.11) | copy-start | bytes 3145732
  459.7 6.9 %copy-start.14 = (f32[64,36,128]{2,1,0:T(8,128)S(1)}, f32[64,36,128]{2,1,0:T(8,128)}, u32[]{:S(2)}) copy-start(f32[64,36,128]{2,1,0:T(8,128)} %copy-done.13) | copy-start | bytes 3538948
  459.7 6.9 %copy-start.25 = (f32[64,32,128]{2,1,0:T(8,128)S(1)}, f32[64,32,128]{2,1,0:T(8,128)}, u32[]{:S(2)}) copy-start(f32[64,32,128]{2,1,0:T(8,128)} %get-tuple-element.81) | copy-start | bytes 3145732
  459.7 6.8 %collective-permute-start.6 = (f32[64,2,128]{2,1,0:T(2,128)S(1)}, f32[64,2,128]{2,1,0:T(2,128)S(1)}, u32[]{:S(2)}, u32[]{:S(2)}) collective-permute-start(f32[64,2,128]{2,1,0:T(2,128)S(1)} %add_add_fusion.2), channel_id=1, source_target_pairs={{0,1},{1,2},{2,3},{3,4},{4,5},{5,6},{6,7},{8,9},{9,10},{10,11},{11... | collective-permute-start | bytes 196616 | tf_op jit(solution)/shard_map/ppermute | solution.py:18
  466.6 53.3 %copy-start.1 = (bf16[1,64,32,256]{3,2,1,0:T(8,128)(2,1)S(1)}, bf16[1,64,32,256]{3,2,1,0:T(8,128)(2,1)}, u32[]{:S(2)}) copy-start(bf16[1,64,32,256]{3,2,1,0:T(8,128)(2,1)} %param.8) | copy-start | bytes 3145732
  (35 other events, 73.7 us)
Sparse Core Ops, SparseCore 0:
  10.2 127.6 all-gather.2
  339.3 115.3 all-reduce.38
  457.0 58.3 all-reduce.40
